TPU v7x, 32 devices: a whole 2x2x4 slice. The times are simulated.
32 devices in a mesh: group: 2 (over y), dp: 16 (over z, x, core).
Axes of the slice: x: 2, y: 2, z: 4, core: 2. Of those that a mesh axis runs over, the one named last changes fastest.
Arguments:
- frames: bfloat16 [2, 64, 128, 84, 336], P('group', 'dp'), may hold values from 0 to 1
- actions: int32 [2, 64, 128], P('group', 'dp'), may hold values from 0 to 17
- rewards: float32 [2, 64, 128], P('group', 'dp'), may hold values from 0 to 0.75
- old_values: float32 [2, 64, 128], P('group', 'dp'), may hold values from -6 to 6
- next_values: float32 [2, 64, 128], P('group', 'dp'), may hold values from -6 to 6
- terminal: int32 [2, 64, 128], P('group', 'dp'), may hold values 0 or 1
- truncated: int32 [2, 64, 128], P('group', 'dp'), may hold values 0 or 1
- behavior_logprob: float32 [2, 64, 128], P('group', 'dp'), may hold values from -3.5 to -2.3
- master: float32 [1695744], P('dp'), may hold values from -2 to 2
- first_moment: float32 [2, 1695744], P('group', 'dp'), may hold values from -1 to 1
- second_moment: float32 [2, 1695744], P('group', 'dp'), may hold values from 0 to 1, as said below
- outer_momentum: float32 [1695744], P('dp'), may hold values from -0.15625 to 0.15625
- step_count: int32 [1], replicated, may hold values from 2 to 20
Outputs:
- grads: float32 [2, 1695744], P('group', 'dp')
- norms: float32 [2], P('group')
- losses: float32 [2], P('group')
- first_new: float32 [2, 1695744], P('group', 'dp')
- second_new: float32 [2, 1695744], P('group', 'dp')
- moved: float32 [1695744], P('dp')
- momentum_new: float32 [1695744], P('dp')
- final: float32 [1695744], P('dp')
- final_low: bfloat16 [1695744], P('dp')
Inputs may be any that keep to these rules, and one draw needn't show every extreme that they name: `second_moment`: entries are positive.
All inputs are finite; a program needn't handle non-finite values. No bound on the sum of `terminal` or of `truncated` on one device may be relied on, other than what follows from the above.
Results may differ from a plain program's by a relative error of at most 0.0011.
The roundings to bfloat16 on the way count: a program that leaves them out, or rounds other values in their place, can miss the bound.
Values may be sent and summed in bfloat16 or wider, within the bound.
No kernel may reach another device: no remote copies, remote signals or barrier semaphores. Data moves between devices by JAX's collectives and lax.ppermute only.
A program may use at most 320 MiB of HBM per device.

v0:
```python
import math
import jax
import jax.numpy as jnp
from jax import lax
from jax.sharding import PartitionSpec as P

C1 = 32
C2 = 64
C3 = 64
HID = 512
ACTIONS = 18
PARAMS = 1693875
BETA_ONE = 0.9
BETA_TWO = 0.999
ADAM_EPSILON = 1e-08
LEARN_RATE = 0.005
WEIGHT_DECAY = 0.01
CLIP_NORM = 0.5
OUTER_RATE = 0.7
OUTER_MOMENTUM = 0.9
DISCOUNT = 0.99
TRACE_DECAY = 0.95
RATIO_CLIP = 0.1
VALUE_COEF = 0.5
ENTROPY_COEF = 0.01


def param_shapes():
    return [
        (8, 8, 4, C1),
        (C1,),
        (4, 4, C1, C2),
        (C2,),
        (3, 3, C2, C3),
        (C3,),
        (49 * C3, HID),
        (HID,),
        (HID, ACTIONS + 1),
        (ACTIONS + 1,),
    ]


def unpack(packed):
    pieces = []
    offset = 0
    for layout in param_shapes():
        length = math.prod(layout)
        pieces.append(packed[offset : offset + length].reshape(layout))
        offset += length
    return pieces


def trajectory_advantages(rewards, values, next_values, terminal, truncated):
    alive = 1.0 - terminal.astype(jnp.float32)
    cutoff = truncated.astype(jnp.float32)
    following = jnp.concatenate([values[:, 1:], next_values[:, -1:]], axis=1)
    following = cutoff * next_values + (1.0 - cutoff) * following
    deltas = rewards + DISCOUNT * alive * following - values
    keeping = DISCOUNT * TRACE_DECAY * alive * (1.0 - cutoff)

    def backward_step(carry, item):
        delta, keep = item
        result = delta + keep * carry
        return (result, result)

    start = jnp.zeros((rewards.shape[0],), jnp.float32)
    _, series = lax.scan(backward_step, start, (deltas.T, keeping.T), reverse=True)
    return series.T


def frame_losses(out, normed, returns, actions, behavior):
    logits = out[:, :ACTIONS]
    value = out[:, ACTIONS]
    log_probs = jax.nn.log_softmax(logits, axis=-1)
    chosen = actions[:, None] == jnp.arange(ACTIONS, dtype=jnp.int32)[None, :]
    taken = jnp.sum(jnp.where(chosen, log_probs, 0.0), axis=-1)
    ratio = jnp.exp(taken - behavior)
    surrogate = jnp.minimum(
        ratio * normed, jnp.clip(ratio, 1.0 - RATIO_CLIP, 1.0 + RATIO_CLIP) * normed
    )
    entropy = -jnp.sum(jnp.exp(log_probs) * log_probs, axis=-1)
    return jnp.sum(-surrogate + 0.5 * VALUE_COEF * (value - returns) ** 2 - ENTROPY_COEF * entropy)


def shifted_conv(inputs, kernel, extent):
    result = 0.0
    for vertical in range(kernel.shape[0]):
        for lateral in range(kernel.shape[1]):
            window = inputs[:, vertical : vertical + extent, lateral : lateral + extent, :]
            result = result + jnp.einsum(
                "bhwc,co->bhwo",
                window,
                kernel[vertical, lateral],
                preferred_element_type=jnp.float32,
            )
    return result


def kernel_grad(inputs, upstream, taps, extent):
    rows_out = []
    for vertical in range(taps):
        line = []
        for lateral in range(taps):
            window = inputs[:, vertical : vertical + extent, lateral : lateral + extent, :]
            line.append(
                jnp.einsum("bhwc,bhwo->co", window, upstream, preferred_element_type=jnp.float32)
            )
        rows_out.append(jnp.stack(line))
    return jnp.stack(rows_out)


def input_grad(upstream, kernel, extent):
    inner_size = upstream.shape[1]
    result = 0.0
    for vertical in range(kernel.shape[0]):
        for lateral in range(kernel.shape[1]):
            term = jnp.einsum(
                "bhwo,co->bhwc",
                upstream,
                kernel[vertical, lateral],
                preferred_element_type=jnp.float32,
            )
            result = result + jnp.pad(
                term,
                (
                    (0, 0),
                    (vertical, extent - inner_size - vertical),
                    (lateral, extent - inner_size - lateral),
                    (0, 0),
                ),
            )
    return result


def column_sum(values):
    return jnp.sum(values.astype(jnp.float32).reshape(-1, values.shape[-1]), axis=0)


def on_device(
    frames,
    actions,
    rewards,
    old_values,
    next_values,
    terminal,
    truncated,
    behavior_logprob,
    master,
    first_moment,
    second_moment,
    outer_momentum,
    step_count,
):
    lanes = lax.axis_size("dp")
    shard_len = master.shape[0]
    weights = lax.all_gather(master.astype(jnp.bfloat16), "dp", axis=0, tiled=True)
    w_one, b_one, w_two, b_two, w_three, b_three, w_dense, b_dense, w_head, b_head = unpack(weights)
    advantage = trajectory_advantages(
        rewards[0], old_values[0], next_values[0], terminal[0], truncated[0]
    )
    envs_here, steps_here = advantage.shape
    batch = envs_here * steps_here
    total_frames = batch * lanes
    first_sum, square_sum = lax.psum((jnp.sum(advantage), jnp.sum(advantage * advantage)), "dp")
    mean = first_sum / total_frames
    spread = square_sum / total_frames - mean * mean
    normed = ((advantage - mean) * lax.rsqrt(spread + 1e-05)).reshape(-1)
    returns = (advantage + old_values[0]).reshape(-1)
    taken_actions = actions[0].reshape(-1)
    behavior = behavior_logprob[0].reshape(-1)
    pixels = (
        frames[0]
        .reshape(batch, 21, 4, 21, 4, 4)
        .transpose(0, 1, 3, 2, 4, 5)
        .reshape(batch, 21, 21, 64)
    )
    kernel_one = w_one.reshape(2, 4, 2, 4, 4, C1).transpose(0, 2, 1, 3, 4, 5).reshape(2, 2, 64, C1)
    conv_one = shifted_conv(pixels, kernel_one, 20) + b_one.astype(jnp.float32)
    act_one = jnp.maximum(conv_one, 0.0).astype(jnp.bfloat16)
    folded_one = (
        act_one.reshape(batch, 10, 2, 10, 2, C1)
        .transpose(0, 1, 3, 2, 4, 5)
        .reshape(batch, 10, 10, 4 * C1)
    )
    kernel_two = (
        w_two.reshape(2, 2, 2, 2, C1, C2).transpose(0, 2, 1, 3, 4, 5).reshape(2, 2, 4 * C1, C2)
    )
    conv_two = shifted_conv(folded_one, kernel_two, 9) + b_two.astype(jnp.float32)
    act_two = jnp.maximum(conv_two, 0.0).astype(jnp.bfloat16)
    conv_three = shifted_conv(act_two, w_three, 7) + b_three.astype(jnp.float32)
    features = jnp.maximum(conv_three, 0.0).astype(jnp.bfloat16).reshape(batch, 49 * C3)
    hidden_pre = jnp.dot(features, w_dense, preferred_element_type=jnp.float32) + b_dense.astype(
        jnp.float32
    )
    hidden = jnp.maximum(hidden_pre, 0.0).astype(jnp.bfloat16)
    out = jnp.dot(hidden, w_head, preferred_element_type=jnp.float32) + b_head.astype(jnp.float32)

    def local_loss(values):
        return frame_losses(values, normed, returns, taken_actions, behavior) / total_frames

    loss_local, pullback = jax.vjp(local_loss, out)
    grad_out = pullback(jnp.ones((), jnp.float32))[0].astype(jnp.bfloat16)
    grad_head = jnp.einsum("bh,bo->ho", hidden, grad_out, preferred_element_type=jnp.float32)
    grad_head_bias = column_sum(grad_out)
    back_hidden = jnp.einsum("bo,ho->bh", grad_out, w_head, preferred_element_type=jnp.float32)
    grad_hidden = jnp.where(hidden_pre > 0, back_hidden, 0.0).astype(jnp.bfloat16)
    grad_dense = jnp.einsum("bi,bh->ih", features, grad_hidden, preferred_element_type=jnp.float32)
    grad_dense_bias = column_sum(grad_hidden)
    back_three = jnp.einsum(
        "bh,ih->bi", grad_hidden, w_dense, preferred_element_type=jnp.float32
    ).reshape(batch, 7, 7, C3)
    grad_conv_three = jnp.where(conv_three > 0, back_three, 0.0).astype(jnp.bfloat16)
    grad_three = kernel_grad(act_two, grad_conv_three, 3, 7)
    grad_three_bias = column_sum(grad_conv_three)
    back_two = input_grad(grad_conv_three, w_three, 9)
    grad_conv_two = jnp.where(conv_two > 0, back_two, 0.0).astype(jnp.bfloat16)
    grad_two_folded = kernel_grad(folded_one, grad_conv_two, 2, 9)
    grad_two = (
        grad_two_folded.reshape(2, 2, 2, 2, C1, C2)
        .transpose(0, 2, 1, 3, 4, 5)
        .reshape(4, 4, C1, C2)
    )
    grad_two_bias = column_sum(grad_conv_two)
    back_folded = input_grad(grad_conv_two, kernel_two, 10)
    back_one = (
        back_folded.reshape(batch, 10, 10, 2, 2, C1)
        .transpose(0, 1, 3, 2, 4, 5)
        .reshape(batch, 20, 20, C1)
    )
    grad_conv_one = jnp.where(conv_one > 0, back_one, 0.0).astype(jnp.bfloat16)
    grad_one_folded = kernel_grad(pixels, grad_conv_one, 2, 20)
    grad_one = (
        grad_one_folded.reshape(2, 2, 4, 4, 4, C1).transpose(0, 2, 1, 3, 4, 5).reshape(8, 8, 4, C1)
    )
    grad_one_bias = column_sum(grad_conv_one)
    pieces = [
        grad_one,
        grad_one_bias,
        grad_two,
        grad_two_bias,
        grad_three,
        grad_three_bias,
        grad_dense,
        grad_dense_bias,
        grad_head,
        grad_head_bias,
    ]
    padding = jnp.zeros((shard_len * lanes - PARAMS,), jnp.float32)
    grad_flat = jnp.concatenate([piece.reshape(-1) for piece in pieces] + [padding])
    summed, loss_total = lax.psum((grad_flat, loss_local), "dp")
    norm = jnp.sqrt(jnp.sum(summed * summed))
    owned = lax.dynamic_slice_in_dim(summed, lax.axis_index("dp") * shard_len, shard_len, 0)
    factor = jnp.minimum(1.0, CLIP_NORM / (norm + 1e-06))
    clipped = owned * factor
    moment_step = step_count[0].astype(jnp.float32)
    first_next = BETA_ONE * first_moment[0] + (1.0 - BETA_ONE) * clipped
    second_next = BETA_TWO * second_moment[0] + (1.0 - BETA_TWO) * clipped * clipped
    first_hat = first_next / (1.0 - jnp.power(BETA_ONE, moment_step))
    second_hat = second_next / (1.0 - jnp.power(BETA_TWO, moment_step))
    inner = master - LEARN_RATE * (
        first_hat / (jnp.sqrt(second_hat) + ADAM_EPSILON) + WEIGHT_DECAY * master
    )
    moved = lax.psum(master - inner, "group") / lax.axis_size("group")
    momentum_next = OUTER_MOMENTUM * outer_momentum + moved
    final = master - OUTER_RATE * (moved + OUTER_MOMENTUM * momentum_next)
    return (
        clipped[None],
        norm.reshape(1),
        loss_total.reshape(1),
        first_next[None],
        second_next[None],
        moved,
        momentum_next,
        final,
        final.astype(jnp.bfloat16),
    )


def solution(mesh):
    return jax.shard_map(
        on_device,
        mesh=mesh,
        in_specs=(
            P("group", "dp", None, None, None),
            P("group", "dp", None),
            P("group", "dp", None),
            P("group", "dp", None),
            P("group", "dp", None),
            P("group", "dp", None),
            P("group", "dp", None),
            P("group", "dp", None),
            P("dp"),
            P("group", "dp"),
            P("group", "dp"),
            P("dp"),
            P(),
        ),
        out_specs=(
            P("group", "dp"),
            P("group"),
            P("group"),
            P("group", "dp"),
            P("group", "dp"),
            P("dp"),
            P("dp"),
            P("dp"),
            P("dp"),
        ),
        check_vma=False,
    )
```

profile of v0, /device:TPU:0, one launch (start us, length us, event | category | flops | bytes accessed | tf_op | source)
XLA Modules:
  0.0 1024.8 jit_solution(7701893610544286102)
XLA Ops:
  11.9 9.6 while.17
  24.1 37.2 %all-reduce.15 = (f32[]{:T(128)}, f32[]{:T(128)}) all-reduce(f32[]{:T(128)} %get-tuple-element.174, f32[]{:T(128)} %reduce_sum.128), channel_id=1, replica_groups=mesh['group'=2,'dp'=16] {'dp'}, use_global_device_ids=true, to_apply=%region_8.9 | all-reduce | flops 2 | bytes 16 | tf_op jit(solution)/shard_map/psum | solution.py:164
  63.9 21.7 %copy.91 = bf16[1,4,128,84,336]{2,1,4,3,0:T(4,128)(2,1)} copy(bf16[1,4,128,84,336]{2,4,3,1,0:T(8,128)(2,1)} %param.15) | data formatting | bytes 57802752 | tf_op args[0]
  85.7 50.5 %reshape_squeeze.8 = bf16[512,21,4,21,4,4]{0,5,4,3,2,1:T(4,128)(2,1)} reshape(bf16[1,4,128,84,336]{2,1,4,3,0:T(4,128)(2,1)} %copy.91) | data formatting | bytes 57802752 | tf_op jit(solution)/shard_map/reshape;squeeze | solution.py:173
  136.1 20.4 %copy.92 = bf16[512,21,21,4,4,4]{0,5,4,3,2,1:T(4,128)(2,1)} copy(bf16[512,21,21,4,4,4]{0,5,4,2,3,1:T(4,128)(2,1)} %bitcast.500) | data formatting | bytes 57802752 | tf_op jit(solution)/shard_map/transpose | solution.py:174
  156.6 45.4 %reshape.158 = bf16[512,21,21,64]{0,3,2,1:T(8,128)(2,1)} reshape(bf16[512,21,21,4,4,4]{0,5,4,3,2,1:T(4,128)(2,1)} %copy.92) | data formatting | bytes 57802752 | tf_op jit(solution)/shard_map/reshape | solution.py:175
  202.0 70.1 %reduce.5 = bf16[16,105984]{1,0:T(8,128)(2,1)S(1)} reduce(bf16[16,1,105984]{2,1,0:T(2,128)(2,1)} %all-gather.3.cloned.1.call-done, bf16[]{:T(256)} %constant.178), dimensions={1}, to_apply=%all-gather.reduce_sub_computation | reduce | bytes 6782978 | tf_op jit(solution)/shard_map/all_gather | solution.py:156
  272.0 6.8 reshape.177
  286.6 3.2 slice.266
  289.8 3.3 dot_general.189
  293.1 3.2 reshape.165
  296.5 19.2 %fusion.4 = f32[512,20,20,32]{0,3,2,1:T(8,128)} fusion(bf16[512,21,21,64]{0,3,2,1:T(8,128)(2,1)} %reshape.158, bf16[2,2,64,32]{3,2,1,0:T(8,128)(2,1)S(1)} %bitcast.516), kind=kOutput, calls=%fused_computation.12 | convolution fusion | flops 838860800 | bytes 52445184 | tf_op jit(solution)/shard_map/bhwc,co->bhwo/dot_general | solution.py:90
  315.7 19.1 %fusion.8 = f32[512,20,20,32]{0,3,2,1:T(8,128)} fusion(bf16[512,21,21,64]{0,3,2,1:T(8,128)(2,1)} %reshape.158, bf16[2,2,64,32]{3,2,1,0:T(8,128)(2,1)S(1)} %bitcast.517), kind=kOutput, calls=%fused_computation.16 | convolution fusion | flops 838860800 | bytes 52445184 | tf_op jit(solution)/shard_map/bhwc,co->bhwo/dot_general | solution.py:90
  334.7 20.3 %fusion.12 = f32[512,20,20,32]{0,3,2,1:T(8,128)} fusion(bf16[512,21,21,64]{0,3,2,1:T(8,128)(2,1)} %reshape.158, bf16[2,2,64,32]{3,2,1,0:T(8,128)(2,1)S(1)} %bitcast.518), kind=kOutput, calls=%fused_computation.20 | convolution fusion | flops 838860800 | bytes 52445184 | tf_op jit(solution)/shard_map/bhwc,co->bhwo/dot_general | solution.py:90
  355.2 46.6 %maximum_convert_fusion = (bf16[512,20,20,32]{0,3,2,1:T(8,128)(2,1)}, f32[512,20,20,32]{0,3,2,1:T(8,128)}) fusion(f32[32]{0:T(128)S(1)} %slice_convert_fusion.4, f32[512,20,20,32]{0,3,2,1:T(8,128)} %fusion.4, f32[512,20,20,32]{0,3,2,1:T(8,128)} %fusion.8, f32[512,20,20,32]{0,3,2,1:T(8,128)} %fusion.12, bf16[512,21,21,64]{0,3,2,1:T(8,128)(2,1)} %reshape.158, ...), kind=kOutput, calls=%fused_computation.8 | convolution fusion | flops 878182400 | bytes 144196096 | tf_op jit(solution)/shard_map/bhwc,co->bhwo/dot_general | solution.py:90
  401.8 6.4 copy.98
  408.2 5.4 fusion.66
  413.6 5.8 fusion.64
  419.4 4.9 fusion.62
  424.4 25.2 %maximum_convert_fusion.1 = (bf16[512,9,9,64]{0,3,2,1:T(8,128)(2,1)}, f32[512,9,9,64]{0,3,2,1:T(8,128)}) fusion(f32[64]{0:T(128)S(1)} %get-tuple-element.168, bf16[512,10,10,128]{0,3,2,1:T(8,128)(2,1)} %bitcast.489, bf16[2,2,128,64]{3,2,1,0:T(8,128)(2,1)S(1)} %bitcast.510, f32[512,9,9,64]{0,3,2,1:T(8,128)} %fusion.66, f32[512,9,9,64]{0,3,2,1:T(8,128)} %fusion.62, ...), kind=kOutput, calls=%fused_computation.30 | convolution fusion | flops 695402496 | bytes 60916224 | tf_op jit(solution)/shard_map/bhwc,co->bhwo/dot_general | solution.py:90
  449.6 5.8 fusion.21
  455.4 3.7 fusion.23
  459.1 3.7 fusion.25
  462.8 3.7 fusion.27
  466.5 3.7 fusion.29
  470.2 3.7 fusion.31
  473.9 3.7 fusion.33
  477.5 3.8 fusion.35
  481.6 18.7 %fusion.41 = (u8[512,7,64]{0,2,1:T(8,128)(4,1)S(1)}, bf16[512,7,7,64]{0,3,2,1:T(8,128)(2,1)S(1)}) fusion(f32[64]{0:T(128)S(1)} %copy-done.39, f32[512,7,7,64]{0,3,2,1:T(8,128)} %fusion.21, f32[512,7,7,64]{0,3,2,1:T(8,128)} %fusion.23, f32[512,7,7,64]{0,3,2,1:T(8,128)} %fusion.25, f32[512,7,7,64]{0,3,2,1:T(8,128)} %fusion.27, f32[512,7,7,64]{0,3,2,1:T(8,128)} %fusion.29, ...), kind=kOutput, calls=%fused_computation.59 | convolution fusion | flops 229376000 | bytes 58049024 | tf_op jit(solution)/shard_map/bhwc,co->bhwo/dot_general | solution.py:90
  508.6 2.9 convert_reduce_fusion.3
  525.7 4.5 convolution_bitcast_fusion
  530.3 3.7 fusion.67
  534.0 4.1 fusion.68
  538.1 3.6 fusion.69
  541.7 3.6 fusion.70
  545.3 3.6 fusion.73
  548.9 5.4 fusion.74
  554.3 5.5 fusion.72
  559.8 5.4 fusion.71
  565.2 5.5 fusion.20
  570.7 22.1 %convert_reduce_fusion.2 = (f32[64]{0:T(128)}, bf16[512,9,9,64]{0,3,2,1:T(8,128)(2,1)S(1)}) fusion(bf16[512,7,7,64]{0,3,2,1:T(8,128)(2,1)S(1)} %get-tuple-element.184, bf16[3,3,64,64]{3,2,1,0:T(8,128)(2,1)S(1)} %reshape.163, f32[512,9,9,64]{0,3,2,1:T(8,128)} %fusion.74, f32[512,7,7,64]{0,3,2,1:T(8,128)} %fusion.73, f32[512,9,9,64]{0,3,2,1:T(8,128)} %fusion.72, ...), kind=kOutput, calls=%fused_computation.28 | convolution fusion | flops 247988160 | bytes 73089280 | tf_op jit(solution)/shard_map/jit(_pad)/pad | solution.py:123
  592.8 8.2 fusion.99
  601.0 6.6 fusion.98
  607.7 3.5 fusion.97
  611.2 3.5 fusion.96
  614.7 8.8 fusion.61
  623.5 8.8 fusion.63
  632.3 8.7 fusion.65
  641.0 9.4 convert_reduce_fusion
  650.4 28.9 %add_add_fusion = bf16[512,10,10,128]{0,3,2,1:T(8,128)(2,1)} fusion(f32[512,9,9,128]{0,3,2,1:T(8,128)} %fusion.65, f32[512,9,9,128]{0,3,2,1:T(8,128)} %fusion.63, f32[512,9,9,128]{0,3,2,1:T(8,128)} %fusion.61, bf16[512,9,9,64]{0,3,2,1:T(8,128)(2,1)} %copy-done.1, bf16[2,2,128,64]{3,2,1,0:T(8,128)(2,1)S(1)} %bitcast.514), kind=kOutput, calls=%fused_computation.7 | convolution fusion | flops 705691648 | bytes 82149376 | tf_op jit(solution)/shard_map/jit(_pad)/pad | solution.py:123
  679.3 6.1 copy.129
  685.4 8.3 convert_reduce_fusion.1
  693.7 15.2 %fusion.52 = f32[64,32]{0,1:T(8,128)S(1)} fusion(bf16[512,20,20,32]{0,3,2,1:T(8,128)(2,1)} %get-tuple-element.166, bf16[512,21,21,64]{0,3,2,1:T(8,128)(2,1)} %reshape.158), kind=kOutput, calls=%fused_computation.76 | convolution fusion | flops 838860800 | bytes 39329792 | tf_op jit(solution)/shard_map/bhwc,bhwo->co/dot_general | solution.py:106
  708.9 15.0 %fusion.49 = f32[64,32]{0,1:T(8,128)S(1)} fusion(bf16[512,20,20,32]{0,3,2,1:T(8,128)(2,1)} %get-tuple-element.166, bf16[512,21,21,64]{0,3,2,1:T(8,128)(2,1)} %reshape.158), kind=kOutput, calls=%fused_computation.75 | convolution fusion | flops 838860800 | bytes 39329792 | tf_op jit(solution)/shard_map/bhwc,bhwo->co/dot_general | solution.py:106
  723.9 15.4 %fusion.46 = f32[64,32]{0,1:T(8,128)S(1)} fusion(bf16[512,20,20,32]{0,3,2,1:T(8,128)(2,1)} %get-tuple-element.166, bf16[512,21,21,64]{0,3,2,1:T(8,128)(2,1)} %reshape.158), kind=kOutput, calls=%fused_computation.74 | convolution fusion | flops 838860800 | bytes 39329792 | tf_op jit(solution)/shard_map/bhwc,bhwo->co/dot_general | solution.py:106
  739.4 15.5 %fusion.43 = f32[64,32]{0,1:T(8,128)S(1)} fusion(bf16[512,20,20,32]{0,3,2,1:T(8,128)(2,1)} %get-tuple-element.166, bf16[512,21,21,64]{0,3,2,1:T(8,128)(2,1)} %reshape.158), kind=kOutput, calls=%fused_computation.73 | convolution fusion | flops 838860800 | bytes 39329792 | tf_op jit(solution)/shard_map/bhwc,bhwo->co/dot_general | solution.py:106
  755.5 7.2 copy.220
  763.4 62.0 %concatenate.13 = f32[1695744]{0:T(1024)} concatenate(f32[8192]{0:T(1024)S(1)} %reshape_reshape.14, f32[32]{0:T(128)S(1)} %get-tuple-element.165, f32[32768]{0:T(1024)S(1)} %reshape_reshape.15, f32[64]{0:T(128)S(1)} %copy-done.38, f32[36864]{0:T(1024)S(1)} %reshape.171, f32[64]{0:T(128)S(1)} %copy-done.40, f32[1605632]{0:T(1024)} %bitcast.504, f32[512]{0:T(512)S(1)} %copy-done.30, ...), dimensions={0} | concatenate | bytes 13565952 | tf_op jit(solution)/shard_map/concatenate | solution.py:249
  826.6 2.5 multiply_reduce_fusion.1
  829.1 140.4 %all-reduce.19.cloned.1.call-done = f32[1695744]{0:T(1024)} async-done(((f32[1695744]{0:T(1024)}), f32[1695744]{0:T(1024)}) %all-reduce.19.cloned.1.call-update) | async-done | bytes 6782992 | tf_op jit(solution)/shard_map/psum | solution.py:250
  969.4 4.5 multiply_reduce_fusion
  974.6 2.2 subtract_subtract_fusion
  978.2 33.3 %psum.38 = f32[1]{0:T(128)} all-reduce(f32[1]{0:T(128)} %bitcast.155), channel_id=1, replica_groups=mesh['group'=2,'dp'=16] {'dp'}, use_global_device_ids=true, to_apply=%region_19.20 | all-reduce | flops 1 | bytes 8 | tf_op jit(solution)/shard_map/psum | solution.py:250
  1014.7 2.2 fusion.93
  (438 shorter events, 50.5 us)
Async XLA Ops:
  7.2 194.8 %all-gather.3.cloned.1.call-start = ((), (), s32[]{:S(2)}) async-start(), calls=%async_computation.2 | async-start | bytes 7206912 | tf_op jit(solution)/shard_map/all_gather | solution.py:156
  9.3 960.2 %all-reduce.19.cloned.1.call-start = ((), (), s32[]{:S(2)}) async-start(), calls=%async_computation | async-start | bytes 13565952 | tf_op jit(solution)/shard_map/psum | solution.py:250
  22.2 63.5 %copy-start.24 = (f32[128,4]{0,1:T(4,128)}, f32[128,4]{0,1:T(4,128)S(1)}, u32[]{:S(2)}) copy-start(f32[128,4]{0,1:T(4,128)S(1)} %copy.119) | copy-start | bytes 6148
  289.8 6.6 slice-start.8
  408.2 11.2 %copy-start = (bf16[512,10,2,10,2,32]{0,5,4,2,3,1:T(8,128)(2,1)}, bf16[512,10,2,10,2,32]{0,5,4,2,3,1:T(8,128)(2,1)S(1)}, u32[]{:S(2)}) copy-start(bf16[512,10,2,10,2,32]{0,5,4,2,3,1:T(8,128)(2,1)S(1)} %copy.98) | copy-start | bytes 39321604
  449.6 5.8 slice-start.4
  449.6 5.8 slice-start.5
  477.5 3.8 copy-start.22
  477.5 4.1 copy-start.39
  500.4 1.9 copy-start.4
  500.4 1.9 copy-start.37
  502.3 2.0 copy-start.41
  502.3 2.3 copy-start.35
  502.3 2.9 copy-start.27
  502.3 3.0 copy-start.25
  502.3 3.0 copy-start.32
  502.3 6.3 copy-start.3
  505.3 0.7 copy-start.28
  506.6 4.9 slice-start.6
  508.6 2.9 slice-start.7
  592.8 39.5 %copy-start.1 = (bf16[512,9,9,64]{0,3,2,1:T(8,128)(2,1)}, bf16[512,9,9,64]{0,3,2,1:T(8,128)(2,1)S(1)}, u32[]{:S(2)}) copy-start(bf16[512,9,9,64]{0,3,2,1:T(8,128)(2,1)S(1)} %get-tuple-element.182) | copy-start | bytes 15925252
  592.8 14.8 %slice-start = ((s8[13107200]{0:T(1024)(128)(4,1)}), s8[4194304]{0:T(1024)(128)(4,1)S(1)}, s32[]{:S(2)}) async-start(s8[13107200]{0:T(1024)(128)(4,1)} %bitcast.492), calls=%async_computation.3 | async-start | bytes 8388608
  592.8 14.8 %slice-start.1 = ((s8[13107200]{0:T(1024)(128)(4,1)}), s8[4194304]{0:T(1024)(128)(4,1)S(1)}, s32[]{:S(2)}) async-start(s8[13107200]{0:T(1024)(128)(4,1)} %bitcast.492), calls=%async_computation.4 | async-start | bytes 8388608
  601.0 6.6 slice-start.2
  601.0 6.6 slice-start.3
  739.3 15.6 %copy-start.5 = (f32[512,19]{1,0:T(8,128)S(1)}, f32[512,19]{1,0:T(8,128)}, u32[]{:S(2)}) copy-start(f32[512,19]{1,0:T(8,128)} %fusion.57) | copy-start | bytes 116740
  739.3 15.8 %copy-start.19 = (f32[1,64,64]{2,1,0:T(8,128)S(1)}, f32[1,64,64]{2,1,0:T(8,128)}, u32[]{:S(2)}) copy-start(f32[1,64,64]{2,1,0:T(8,128)} %convolution_bitcast_fusion.1) | copy-start | bytes 49156
  739.3 15.8 %copy-start.20 = (f32[1,64,64]{2,1,0:T(8,128)S(1)}, f32[1,64,64]{2,1,0:T(8,128)}, u32[]{:S(2)}) copy-start(f32[1,64,64]{2,1,0:T(8,128)} %convolution_bitcast_fusion.2) | copy-start | bytes 49156
  739.3 15.8 %copy-start.21 = (f32[1,64,64]{2,1,0:T(8,128)S(1)}, f32[1,64,64]{2,1,0:T(8,128)}, u32[]{:S(2)}) copy-start(f32[1,64,64]{2,1,0:T(8,128)} %convolution_bitcast_fusion.3) | copy-start | bytes 49156
  739.3 15.8 %copy-start.13 = (f32[1,64,64]{2,1,0:T(8,128)S(1)}, f32[1,64,64]{2,1,0:T(8,128)}, u32[]{:S(2)}) copy-start(f32[1,64,64]{2,1,0:T(8,128)} %convolution_bitcast_fusion.4) | copy-start | bytes 49156
  739.4 15.8 %copy-start.14 = (f32[1,64,64]{2,1,0:T(8,128)S(1)}, f32[1,64,64]{2,1,0:T(8,128)}, u32[]{:S(2)}) copy-start(f32[1,64,64]{2,1,0:T(8,128)} %convolution_bitcast_fusion.5) | copy-start | bytes 49156
  739.4 15.8 %copy-start.15 = (f32[1,64,64]{2,1,0:T(8,128)S(1)}, f32[1,64,64]{2,1,0:T(8,128)}, u32[]{:S(2)}) copy-start(f32[1,64,64]{2,1,0:T(8,128)} %convolution_bitcast_fusion.6) | copy-start | bytes 49156
  739.4 15.8 %copy-start.16 = (f32[1,64,64]{2,1,0:T(8,128)S(1)}, f32[1,64,64]{2,1,0:T(8,128)}, u32[]{:S(2)}) copy-start(f32[1,64,64]{2,1,0:T(8,128)} %convolution_bitcast_fusion.7) | copy-start | bytes 49156
  739.4 15.8 %copy-start.17 = (f32[1,64,64]{2,1,0:T(8,128)S(1)}, f32[1,64,64]{2,1,0:T(8,128)}, u32[]{:S(2)}) copy-start(f32[1,64,64]{2,1,0:T(8,128)} %convolution_bitcast_fusion.8) | copy-start | bytes 49156
  739.4 15.8 %copy-start.18 = (f32[1,64,64]{2,1,0:T(8,128)S(1)}, f32[1,64,64]{2,1,0:T(8,128)}, u32[]{:S(2)}) copy-start(f32[1,64,64]{2,1,0:T(8,128)} %convolution_bitcast_fusion.9) | copy-start | bytes 49156
  755.4 7.3 copy-start.9
  755.4 7.3 copy-start.10
  755.4 7.3 copy-start.11
  755.4 7.3 copy-start.12
  755.4 7.9 copy-start.30
  755.4 7.9 copy-start.36
  755.5 7.9 copy-start.38
  755.5 7.9 copy-start.40
  825.4 1.0 copy-start.7
  825.4 1.1 copy-start.8
  825.4 149.2 %copy-start.2 = (f32[105984]{0:T(1024)S(1)}, f32[105984]{0:T(1024)}, u32[]{:S(2)}) copy-start(f32[105984]{0:T(1024)} %param.23) | copy-start | bytes 1271812
  825.5 151.4 %copy-start.23 = (f32[1,4,128]{2,1,0:T(4,128)S(1)}, f32[1,4,128]{2,1,0:T(4,128)}, u32[]{:S(2)}) copy-start(f32[1,4,128]{2,1,0:T(4,128)} %param.18) | copy-start | bytes 6148
  825.5 151.4 %copy-start.26 = (f32[128,4]{0,1:T(4,128)S(1)}, f32[128,4]{0,1:T(4,128)}, u32[]{:S(2)}) copy-start(f32[128,4]{0,1:T(4,128)} %copy-done.24) | copy-start | bytes 6148
  825.5 151.4 %copy-start.29 = (f32[512]{0:T(512)S(1)}, f32[512]{0:T(512)}, u32[]{:S(2)}) copy-start(f32[512]{0:T(512)} %copy-done.28) | copy-start | bytes 6148
  825.5 151.4 %copy-start.31 = (f32[512]{0:T(512)S(1)}, f32[512]{0:T(512)}, u32[]{:S(2)}) copy-start(f32[512]{0:T(512)} %get-tuple-element.141) | copy-start | bytes 6148
  825.5 151.4 %copy-start.33 = (f32[1,4,128]{2,1,0:T(4,128)S(1)}, f32[1,4,128]{2,1,0:T(4,128)}, u32[]{:S(2)}) copy-start(f32[1,4,128]{2,1,0:T(4,128)} %param.22) | copy-start | bytes 6148
  825.5 151.4 %copy-start.34 = (f32[512,1]{0,1:T(1,128)S(1)}, f32[512,1]{0,1:T(1,128)}, u32[]{:S(2)}) copy-start(f32[512,1]{0,1:T(1,128)} %get-tuple-element.169) | copy-start | bytes 6148
  825.5 189.1 %all-reduce.21.cloned.1.call-start = ((), (), s32[]{:S(2)}) async-start(), calls=%async_computation.1 | async-start | bytes 851968 | tf_op jit(solution)/shard_map/psum | solution.py:263
  829.1 185.6 %copy-start.6 = (f32[105984]{0:T(1024)S(1)}, f32[105984]{0:T(1024)}, u32[]{:S(2)}) copy-start(f32[105984]{0:T(1024)} %param.26) | copy-start | bytes 1271812
Sparse Core Ops, SparseCore 0:
  10.7 67.2 all-gather.2
  825.6 143.8 all-reduce.18
  977.0 26.5 all-reduce.20
where the time goes:
time: 1040 us; the launch traced here: 1020 us
  matrix products  418 us (40%)
  local copies, waits for them, and re-layouts  253 us (24%)
  waiting for transfers between devices  140 us (13%)
  other arithmetic  119 us (11%)
  blocking collectives  70.6 us (7%)
  between operations  20.8 us (2%)
    dot_general x17, matrix products, shifted_conv(): jnp.einsum('bhwc,co->bhwo', window, kernel[vertical, lateral], preferred_...  197 us
    psum x1, waiting for transfers between devices, on_device(): summed, loss_total = lax.psum((grad_flat, loss_local), 'dp')  140 us
    dot_general x17, matrix products, kernel_grad(): jnp.einsum('bhwc,bhwo->co', window, upstream, preferred_element_type=jnp....  97.1 us
    all_gather x1, other arithmetic, on_device(): lax.all_gather(master.astype(jnp.bfloat16), 'dp', axis=0, tiled=True)  70.1 us
    pad x5, matrix products, input_grad(): jnp.pad(term, ((0, 0), (vertical, extent - inner_size - vertical), (later...  67.2 us
    concatenate x1, local copies, waits for them, and re-layouts, on_device(): jnp.concatenate([piece.reshape(-1) for piece in pieces] + [padding])  62 us
    another operation x1, local copies, waits for them, and re-layouts, on_device(): pixels = frames[0].reshape(batch, 21, 4, 21, 4, 4).transpose(0, 1, 3, 2,...  50.5 us
    reshape x1, local copies, waits for them, and re-layouts, on_device(): pixels = frames[0].reshape(batch, 21, 4, 21, 4, 4).transpose(0, 1, 3, 2,...  45.4 us
  transfers between devices with their start and end apart: 3, of which 1 were waited for; matrix products, arithmetic and copies ran while one was open for 15% of the time, Pallas kernels for 0%

commit v1 on v0

--- a/solution.py
+++ b/solution.py
@@ -153,7 +153,19 @@
 ):
     lanes = lax.axis_size("dp")
     shard_len = master.shape[0]
-    weights = lax.all_gather(master.astype(jnp.bfloat16), "dp", axis=0, tiled=True)
+
+    def get_steps_all(q_in):
+        v1, small = (jax.lax.axis_size("dp"), jax.lax.axis_index("dp"))
+        r_now, newest = (q_in, 1)
+        while newest < v1:
+            q_next = jax.lax.ppermute(r_now, "dp", [(q, q ^ newest) for q in range(v1)])
+            ready = jnp.concatenate([r_now, q_next], axis=0)
+            arr_out = jnp.concatenate([q_next, r_now], axis=0)
+            r_now = jnp.where(small & newest == 0, ready, arr_out)
+            newest = 2 * newest
+        return r_now
+
+    weights = get_steps_all(master.astype(jnp.bfloat16))
     w_one, b_one, w_two, b_two, w_three, b_three, w_dense, b_dense, w_head, b_head = unpack(weights)
     advantage = trajectory_advantages(
         rewards[0], old_values[0], next_values[0], terminal[0], truncated[0]

time: 1040 us -> 1130 us (1.087)
  other arithmetic: 119 us -> 147 us
  local copies, waits for them, and re-layouts: 253 us -> 281 us
  waiting for transfers between devices: 140 us -> 167 us
    add x128, other arithmetic: 2.43 us -> 90.3 us  [backward_step(): result = delta + keep * carry]
    all_gather x1 -> x0, other arithmetic: 70.1 us -> none  [on_device(): lax.all_gather(master.astype(jnp.bfloat16), 'dp', axis=0, tiled=True)]
    ppermute x0 -> x4, waiting for transfers between devices: none -> 26.5 us  [get_steps_all(): q_next = jax.lax.ppermute(r_now, 'dp', [(q, q ^ newest) for q in range(v1)])]
    concatenate x0 -> x2, local copies, waits for them, and re-layouts: none -> 22.4 us  [get_steps_all(): ready = jnp.concatenate([r_now, q_next], axis=0)]
    select_n x0 -> x2, local copies, waits for them, and re-layouts: none -> 17.2 us  [get_steps_all(): r_now = jnp.where(small & newest == 0, ready, arr_out)]
    select_n x0 -> x4, other arithmetic: none -> 12.6 us  [get_steps_all(): r_now = jnp.where(small & newest == 0, ready, arr_out)]
    unnamed x106 -> x108, local copies, waits for them, and re-layouts: 38.4 us -> 31.4 us
  transfers between devices with their start and end apart: 3 -> 6, of which waited for: 1 -> 4; matrix products, arithmetic and copies ran while one was open for 15% -> 23% of each run, Pallas kernels for 0% -> 0%
where the time goes in v1:
time: 1130 us; the launch traced here: 1110 us
  matrix products  417 us (37%)
  local copies, waits for them, and re-layouts  281 us (25%)
  waiting for transfers between devices  167 us (15%)
  other arithmetic  147 us (13%)
  blocking collectives  63.5 us (6%)
  between operations  21.2 us (2%)
    dot_general x17, matrix products, shifted_conv(): jnp.einsum('bhwc,co->bhwo', window, kernel[vertical, lateral], preferred_...  197 us
    psum x1, waiting for transfers between devices, on_device(): summed, loss_total = lax.psum((grad_flat, loss_local), 'dp')  140 us
    dot_general x17, matrix products, kernel_grad(): jnp.einsum('bhwc,bhwo->co', window, upstream, preferred_element_type=jnp....  96.4 us
    add x128, other arithmetic, backward_step(): result = delta + keep * carry  90.3 us
    pad x5, matrix products, input_grad(): jnp.pad(term, ((0, 0), (vertical, extent - inner_size - vertical), (later...  67.2 us
    concatenate x1, local copies, waits for them, and re-layouts, on_device(): jnp.concatenate([piece.reshape(-1) for piece in pieces] + [padding])  62.3 us
    another operation x1, local copies, waits for them, and re-layouts, on_device(): pixels = frames[0].reshape(batch, 21, 4, 21, 4, 4).transpose(0, 1, 3, 2,...  50.5 us
    reshape x1, local copies, waits for them, and re-layouts, on_device(): pixels = frames[0].reshape(batch, 21, 4, 21, 4, 4).transpose(0, 1, 3, 2,...  45.4 us
  transfers between devices with their start and end apart: 6, of which 4 were waited for; matrix products, arithmetic and copies ran while one was open for 23% of the time, Pallas kernels for 0%

profile of v1, /device:TPU:0, one launch (start us, length us, event | category | flops | bytes accessed | tf_op | source)
XLA Modules:
  0.0 1105.9 jit_solution(8843107259524715852)
XLA Ops:
  10.1 2.9 collective-permute-start.1
  13.0 10.1 collective-permute-done.1
  28.3 15.3 %collective-permute-done.2 = bf16[423936]{0:T(1024)(128)(2,1)S(1)} collective-permute-done((bf16[423936]{0:T(1024)(128)(2,1)S(1)}, bf16[423936]{0:T(1024)(128)(2,1)S(1)}, u32[]{:S(2)}, u32[]{:S(2)}) %collective-permute-start.2) | collective-permute-done | bytes 847904 | tf_op jit(solution)/shard_map/ppermute | solution.py:161
  46.8 94.4 %while.17 = (s32[]{:T(128)}, f32[4]{0:T(128)S(1)}, f32[128,4]{1,0:T(8,128)S(1)}, f32[128,4]{1,0:T(8,128)}, f32[128,4]{1,0:T(8,128)S(1)}, /*index=5*/s32[]{:T(128)}, s32[]{:T(128)}, s32[]{:T(128)}) while((s32[]{:T(128)}, f32[4]{0:T(128)S(1)}, f32[128,4]{1,0:T(8,128)S(1)}, f32[128,4]{1,0:T(8,128)}, f32[128,4]{1,0:T(8,128)S(1)}, ...), condition=%wide.region_1.2_spmd.clone, body=%wide.region_0.1_spmd.clone.sunk | while | flops 16 | bytes 219 | solution.py:67
  143.0 30.1 %all-reduce.15 = (f32[]{:T(128)}, f32[]{:T(128)}) all-reduce(f32[]{:T(128)} %get-tuple-element.174, f32[]{:T(128)} %reduce_sum.128), channel_id=1, replica_groups=mesh['group'=2,'dp'=16] {'dp'}, use_global_device_ids=true, to_apply=%region_8.9 | all-reduce | flops 2 | bytes 16 | tf_op jit(solution)/shard_map/psum | solution.py:176
  175.8 21.7 %copy.97 = bf16[1,4,128,84,336]{2,1,4,3,0:T(4,128)(2,1)} copy(bf16[1,4,128,84,336]{2,4,3,1,0:T(8,128)(2,1)} %param.15) | data formatting | bytes 57802752 | tf_op args[0]
  197.5 50.5 %reshape_squeeze.8 = bf16[512,21,4,21,4,4]{0,5,4,3,2,1:T(4,128)(2,1)} reshape(bf16[1,4,128,84,336]{2,1,4,3,0:T(4,128)(2,1)} %copy.97) | data formatting | bytes 57802752 | tf_op jit(solution)/shard_map/reshape;squeeze | solution.py:185
  248.0 20.2 %copy.98 = bf16[512,21,21,4,4,4]{0,5,4,3,2,1:T(4,128)(2,1)} copy(bf16[512,21,21,4,4,4]{0,5,4,2,3,1:T(4,128)(2,1)} %bitcast.508) | data formatting | bytes 57802752 | tf_op jit(solution)/shard_map/transpose | solution.py:186
  268.1 45.4 %reshape.160 = bf16[512,21,21,64]{0,3,2,1:T(8,128)(2,1)} reshape(bf16[512,21,21,4,4,4]{0,5,4,3,2,1:T(4,128)(2,1)} %copy.98) | data formatting | bytes 57802752 | tf_op jit(solution)/shard_map/reshape | solution.py:187
  313.5 4.9 select_n.103
  318.5 12.2 %copy.91 = bf16[207,4,2,4,4,32]{0,5,4,3,2,1:T(8,128)(2,1)} copy(bf16[207,4,2,4,4,32]{5,4,3,2,1,0:T(4,128)(2,1)} %select_n.103) | data formatting | bytes 3391488 | tf_op jit(solution)/shard_map/jit(_where)/select_n | solution.py:164
  330.7 11.8 %maximum_select_fusion = bf16[1695744]{0:T(1024)(128)(2,1)S(1)} fusion(bf16[847872]{0:T(1024)(128)(2,1)S(1)} %collective-permute-done.3, bf16[847872]{0:T(1024)(128)(2,1)S(1)} %maximum_select_fusion.1, pred[]{:T(512)S(6)} %eq.45), kind=kLoop, calls=%fused_computation.38 | loop fusion | flops 15261696 | bytes 6782977 | tf_op jit(solution)/shard_map/jit(_where)/select_n | solution.py:164
  347.0 3.3 dot_general.189
  350.3 3.3 reshape.166
  353.6 10.0 concatenate.50
  363.6 12.4 %copy.92 = bf16[207,4,2,4,4,32]{0,5,4,3,2,1:T(8,128)(2,1)} copy(bf16[207,4,2,4,4,32]{5,4,3,2,1,0:T(4,128)(2,1)} %concatenate.50) | data formatting | bytes 3391488 | tf_op jit(solution)/shard_map/concatenate | solution.py:162
  378.4 19.0 %fusion.4 = f32[32,512,20,20]{1,0,3,2:T(8,128)} fusion(bf16[512,21,21,64]{0,3,2,1:T(8,128)(2,1)} %reshape.160, bf16[2,2,64,32]{3,2,1,0:T(8,128)(2,1)S(1)} %bitcast.524), kind=kOutput, calls=%fused_computation.10 | convolution fusion | flops 838860800 | bytes 52445184 | tf_op jit(solution)/shard_map/bhwc,co->bhwo/dot_general | solution.py:90
  397.4 19.1 %fusion.8 = f32[32,512,20,20]{1,0,3,2:T(8,128)} fusion(bf16[512,21,21,64]{0,3,2,1:T(8,128)(2,1)} %reshape.160, bf16[2,2,64,32]{3,2,1,0:T(8,128)(2,1)S(1)} %bitcast.525), kind=kOutput, calls=%fused_computation.14 | convolution fusion | flops 838860800 | bytes 52445184 | tf_op jit(solution)/shard_map/bhwc,co->bhwo/dot_general | solution.py:90
  416.5 20.1 %fusion.12 = f32[32,512,20,20]{1,0,3,2:T(8,128)} fusion(bf16[512,21,21,64]{0,3,2,1:T(8,128)(2,1)} %reshape.160, bf16[2,2,64,32]{3,2,1,0:T(8,128)(2,1)S(1)} %bitcast.526), kind=kOutput, calls=%fused_computation.18 | convolution fusion | flops 838860800 | bytes 52445184 | tf_op jit(solution)/shard_map/bhwc,co->bhwo/dot_general | solution.py:90
  436.8 46.4 %maximum_convert_fusion = (bf16[32,512,20,20]{1,0,3,2:T(8,128)(2,1)}, f32[32,512,20,20]{1,0,3,2:T(8,128)}) fusion(f32[32]{0:T(128)S(1)} %slice_convert_fusion.4, f32[32,512,20,20]{1,0,3,2:T(8,128)} %fusion.4, f32[32,512,20,20]{1,0,3,2:T(8,128)} %fusion.8, f32[32,512,20,20]{1,0,3,2:T(8,128)} %fusion.12, bf16[512,21,21,64]{0,3,2,1:T(8,128)(2,1)} %reshape.160, ...), kind=kOutput, calls=%fused_computation.3 | convolution fusion | flops 878182400 | bytes 144196096 | tf_op jit(solution)/shard_map/bhwc,co->bhwo/dot_general | solution.py:90
  483.2 6.4 copy.102
  489.6 5.3 fusion.66
  494.9 5.7 fusion.64
  500.7 5.3 fusion.62
  506.1 25.0 %maximum_convert_fusion.1 = (bf16[512,9,9,64]{0,3,2,1:T(8,128)(2,1)}, f32[512,9,9,64]{0,3,2,1:T(8,128)}) fusion(f32[64]{0:T(128)S(1)} %get-tuple-element.168, bf16[512,10,10,128]{0,3,2,1:T(8,128)(2,1)} %bitcast.497, bf16[2,2,128,64]{3,2,1,0:T(8,128)(2,1)S(1)} %bitcast.518, f32[512,9,9,64]{0,3,2,1:T(8,128)} %fusion.66, f32[512,9,9,64]{0,3,2,1:T(8,128)} %fusion.62, ...), kind=kOutput, calls=%fused_computation.28 | convolution fusion | flops 695402496 | bytes 60916224 | tf_op jit(solution)/shard_map/bhwc,co->bhwo/dot_general | solution.py:90
  531.2 5.8 fusion.23
  537.0 3.7 fusion.25
  540.7 3.7 fusion.27
  544.4 3.7 fusion.29
  548.1 3.7 fusion.31
  551.8 3.8 fusion.33
  555.6 3.7 fusion.35
  559.3 3.9 fusion.37
  563.4 18.7 %fusion.39 = (u8[512,7,64]{0,2,1:T(8,128)(4,1)S(1)}, bf16[512,7,7,64]{0,3,2,1:T(8,128)(2,1)S(1)}) fusion(f32[64]{0:T(128)S(1)} %copy-done.41, bf16[512,9,9,64]{0,3,2,1:T(8,128)(2,1)} %get-tuple-element.177, bf16[3,3,64,64]{3,2,1,0:T(8,128)(2,1)S(1)} %reshape.164, f32[512,7,7,64]{0,3,2,1:T(8,128)} %fusion.23, f32[512,7,7,64]{0,3,2,1:T(8,128)} %fusion.25, ...), kind=kOutput, calls=%fused_computation.59 | convolution fusion | flops 229376000 | bytes 58049024 | tf_op jit(solution)/shard_map/bhwc,co->bhwo/dot_general | solution.py:90
  590.2 2.9 convert_reduce_fusion.2
  607.4 4.6 convolution_bitcast_fusion
  612.0 3.6 fusion.67
  615.6 4.1 fusion.68
  619.8 3.6 fusion.69
  623.3 3.7 fusion.70
  627.0 3.6 fusion.73
  630.6 5.5 fusion.74
  636.1 5.5 fusion.72
  641.6 5.5 fusion.71
  647.1 5.5 fusion.20
  652.6 22.0 %convert_reduce_fusion.1 = (f32[64]{0:T(128)}, bf16[512,9,9,64]{0,3,2,1:T(8,128)(2,1)S(1)}) fusion(bf16[512,7,7,64]{0,3,2,1:T(8,128)(2,1)S(1)} %get-tuple-element.184, bf16[3,3,64,64]{3,2,1,0:T(8,128)(2,1)S(1)} %reshape.164, f32[512,9,9,64]{0,3,2,1:T(8,128)} %fusion.74, f32[512,7,7,64]{0,3,2,1:T(8,128)} %fusion.73, f32[512,9,9,64]{0,3,2,1:T(8,128)} %fusion.72, ...), kind=kOutput, calls=%fused_computation.26 | convolution fusion | flops 247988160 | bytes 73089280 | tf_op jit(solution)/shard_map/jit(_pad)/pad | solution.py:123
  674.7 8.2 fusion.101
  682.9 6.6 fusion.100
  689.5 3.5 fusion.99
  695.9 8.8 fusion.61
  704.7 8.8 fusion.63
  713.5 8.8 fusion.65
  722.3 28.6 %add_add_fusion = bf16[512,10,10,128]{0,3,2,1:T(8,128)(2,1)} fusion(f32[512,9,9,128]{0,3,2,1:T(8,128)} %fusion.65, f32[512,9,9,128]{0,3,2,1:T(8,128)} %fusion.63, f32[512,9,9,128]{0,3,2,1:T(8,128)} %fusion.61, bf16[512,9,9,64]{0,3,2,1:T(8,128)(2,1)} %copy-done.1, bf16[2,2,128,64]{3,2,1,0:T(8,128)(2,1)S(1)} %bitcast.522), kind=kOutput, calls=%fused_computation.6 | convolution fusion | flops 705691648 | bytes 82149376 | tf_op jit(solution)/shard_map/jit(_pad)/pad | solution.py:123
  750.9 6.1 copy.133
  757.1 16.9 %convert_reduce_fusion = (f32[32]{0:T(128)S(1)}, bf16[512,20,20,32]{0,3,2,1:T(8,128)(2,1)}) fusion(bf16[512,20,20,32]{0,3,2,1:T(8,128)(2,1)S(1)} %bitcast.511, f32[32,512,20,20]{1,0,3,2:T(8,128)} %get-tuple-element.176), kind=kLoop, calls=%fused_computation.4 | loop fusion | flops 26214368 | bytes 52428928 | tf_op jit(solution)/shard_map/reduce_sum | solution.py:136
  774.0 15.0 %fusion.50 = f32[64,32]{0,1:T(8,128)S(1)} fusion(bf16[512,20,20,32]{0,3,2,1:T(8,128)(2,1)} %get-tuple-element.166, bf16[512,21,21,64]{0,3,2,1:T(8,128)(2,1)} %reshape.160), kind=kOutput, calls=%fused_computation.76 | convolution fusion | flops 838860800 | bytes 39329792 | tf_op jit(solution)/shard_map/bhwc,bhwo->co/dot_general | solution.py:106
  789.0 15.2 %fusion.47 = f32[64,32]{0,1:T(8,128)S(1)} fusion(bf16[512,20,20,32]{0,3,2,1:T(8,128)(2,1)} %get-tuple-element.166, bf16[512,21,21,64]{0,3,2,1:T(8,128)(2,1)} %reshape.160), kind=kOutput, calls=%fused_computation.75 | convolution fusion | flops 838860800 | bytes 39329792 | tf_op jit(solution)/shard_map/bhwc,bhwo->co/dot_general | solution.py:106
  804.2 15.4 %fusion.44 = f32[64,32]{0,1:T(8,128)S(1)} fusion(bf16[512,20,20,32]{0,3,2,1:T(8,128)(2,1)} %get-tuple-element.166, bf16[512,21,21,64]{0,3,2,1:T(8,128)(2,1)} %reshape.160), kind=kOutput, calls=%fused_computation.74 | convolution fusion | flops 838860800 | bytes 39329792 | tf_op jit(solution)/shard_map/bhwc,bhwo->co/dot_general | solution.py:106
  819.7 15.5 %fusion.41 = f32[64,32]{0,1:T(8,128)S(1)} fusion(bf16[512,20,20,32]{0,3,2,1:T(8,128)(2,1)} %get-tuple-element.166, bf16[512,21,21,64]{0,3,2,1:T(8,128)(2,1)} %reshape.160), kind=kOutput, calls=%fused_computation.73 | convolution fusion | flops 838860800 | bytes 39329792 | tf_op jit(solution)/shard_map/bhwc,bhwo->co/dot_general | solution.py:106
  835.8 7.3 copy.224
  843.8 62.3 %concatenate.56 = f32[1695744]{0:T(1024)} concatenate(f32[8192]{0:T(1024)S(1)} %reshape_reshape.11, f32[32]{0:T(128)S(1)} %get-tuple-element.165, f32[32768]{0:T(1024)S(1)} %reshape_reshape.12, f32[64]{0:T(128)S(1)} %copy-done.40, f32[36864]{0:T(1024)S(1)} %reshape.172, f32[64]{0:T(128)S(1)} %copy-done.42, f32[1605632]{0:T(1024)} %bitcast.512, f32[512]{0:T(512)S(1)} %copy-done.32, ...), dimensions={0} | concatenate | bytes 13565952 | tf_op jit(solution)/shard_map/concatenate | solution.py:261
  909.7 140.4 %all-reduce.19.cloned.1.call-done = f32[1695744]{0:T(1024)} async-done(((f32[1695744]{0:T(1024)}), f32[1695744]{0:T(1024)}) %all-reduce.19.cloned.1.call-update) | async-done | bytes 6782992 | tf_op jit(solution)/shard_map/psum | solution.py:262
  1050.1 4.5 multiply_reduce_fusion
  1058.9 33.3 %psum.38 = f32[1]{0:T(128)} all-reduce(f32[1]{0:T(128)} %bitcast.157), channel_id=1, replica_groups=mesh['group'=2,'dp'=16] {'dp'}, use_global_device_ids=true, to_apply=%region_19.20 | all-reduce | flops 1 | bytes 8 | tf_op jit(solution)/shard_map/psum | solution.py:262
  (449 shorter events, 151.4 us)
Async XLA Ops:
  7.2 134.6 %copy-start.24 = (f32[1,4,128]{2,1,0:T(4,128)S(1)}, f32[1,4,128]{2,1,0:T(4,128)}, u32[]{:S(2)}) copy-start(f32[1,4,128]{2,1,0:T(4,128)} %param.18) | copy-start | bytes 6148
  7.2 1043.0 %all-reduce.19.cloned.1.call-start = ((), (), s32[]{:S(2)}) async-start(), calls=%async_computation | async-start | bytes 13565952 | tf_op jit(solution)/shard_map/psum | solution.py:262
  8.3 1.6 collective-permute-start
  10.1 13.0 %collective-permute-start.1 = (bf16[211968]{0:T(1024)(128)(2,1)S(1)}, bf16[211968]{0:T(1024)(128)(2,1)S(1)}, u32[]{:S(2)}, u32[]{:S(2)}) collective-permute-start(bf16[211968]{0:T(1024)(128)(2,1)S(1)} %maximum_select_fusion.3), channel_id=1, source_target_pairs={{0,2},{1,3},{2,0},{3,1},{4,6},{5,7},{6,4},{7,5},{8,10},{9,11},{10,... | collective-permute-start | bytes 1271816 | tf_op jit(solution)/shard_map/ppermute | solution.py:161
  23.3 20.4 %collective-permute-start.2 = (bf16[423936]{0:T(1024)(128)(2,1)S(1)}, bf16[423936]{0:T(1024)(128)(2,1)S(1)}, u32[]{:S(2)}, u32[]{:S(2)}) collective-permute-start(bf16[423936]{0:T(1024)(128)(2,1)S(1)} %maximum_select_fusion.2), channel_id=1, source_target_pairs={{0,4},{1,5},{2,6},{3,7},{4,0},{5,1},{6,2},{7,3},{8,12},{9,13},{10,... | collective-permute-start | bytes 2543624 | tf_op jit(solution)/shard_map/ppermute | solution.py:161
  44.1 286.6 %collective-permute-start.3 = (bf16[847872]{0:T(1024)(128)(2,1)S(1)}, bf16[847872]{0:T(1024)(128)(2,1)S(1)}, u32[]{:S(2)}, u32[]{:S(2)}) collective-permute-start(bf16[847872]{0:T(1024)(128)(2,1)S(1)} %maximum_select_fusion.1), channel_id=1, source_target_pairs={{0,8},{1,9},{2,10},{3,11},{4,12},{5,13},{6,14},{7,15},{8,0},{9,1},... | collective-permute-start | bytes 5087240 | tf_op jit(solution)/shard_map/ppermute | solution.py:161
  141.8 55.7 %copy-start.26 = (f32[128,4]{0,1:T(4,128)}, f32[128,4]{0,1:T(4,128)S(1)}, u32[]{:S(2)}) copy-start(f32[128,4]{0,1:T(4,128)S(1)} %copy.123) | copy-start | bytes 6148
  330.7 14.4 %copy-start.3 = (bf16[847872]{0:T(1024)(128)(2,1)}, bf16[847872]{0:T(1024)(128)(2,1)S(1)}, u32[]{:S(2)}) copy-start(bf16[847872]{0:T(1024)(128)(2,1)S(1)} %collective-permute-done.3) | copy-start | bytes 5087236
  363.6 12.4 %copy-start.2 = (bf16[207,4,2,4,4,32]{0,5,4,3,2,1:T(8,128)(2,1)S(1)}, bf16[207,4,2,4,4,32]{0,5,4,3,2,1:T(8,128)(2,1)}, u32[]{:S(2)}) copy-start(bf16[207,4,2,4,4,32]{0,5,4,3,2,1:T(8,128)(2,1)} %copy.91) | copy-start | bytes 5087236
  489.6 11.1 %copy-start = (bf16[512,10,2,10,2,32]{0,5,4,2,3,1:T(8,128)(2,1)}, bf16[512,10,2,10,2,32]{0,5,4,2,3,1:T(8,128)(2,1)S(1)}, u32[]{:S(2)}) copy-start(bf16[512,10,2,10,2,32]{0,5,4,2,3,1:T(8,128)(2,1)S(1)} %copy.102) | copy-start | bytes 39321604
  531.2 5.8 slice-start.4
  531.2 5.8 slice-start.5
  559.3 3.9 copy-start.23
  559.3 4.1 copy-start.41
  582.1 1.9 copy-start.6
  582.1 1.9 copy-start.39
  584.0 2.0 copy-start.43
  584.0 2.3 copy-start.37
  584.0 2.9 copy-start.29
  584.0 2.9 copy-start.27
  584.0 2.9 copy-start.34
  584.1 6.2 copy-start.5
  587.0 0.6 copy-start.30
  588.3 4.9 slice-start.6
  590.2 2.9 slice-start.7
  674.7 38.8 %copy-start.1 = (bf16[512,9,9,64]{0,3,2,1:T(8,128)(2,1)}, bf16[512,9,9,64]{0,3,2,1:T(8,128)(2,1)S(1)}, u32[]{:S(2)}) copy-start(bf16[512,9,9,64]{0,3,2,1:T(8,128)(2,1)S(1)} %get-tuple-element.182) | copy-start | bytes 15925252
  674.7 14.8 %slice-start = ((s8[13107200]{0:T(1024)(128)(4,1)}), s8[4194304]{0:T(1024)(128)(4,1)S(1)}, s32[]{:S(2)}) async-start(s8[13107200]{0:T(1024)(128)(4,1)} %bitcast.500), calls=%async_computation.2 | async-start | bytes 8388608
  674.7 14.8 %slice-start.1 = ((s8[13107200]{0:T(1024)(128)(4,1)}), s8[4194304]{0:T(1024)(128)(4,1)S(1)}, s32[]{:S(2)}) async-start(s8[13107200]{0:T(1024)(128)(4,1)} %bitcast.500), calls=%async_computation.3 | async-start | bytes 8388608
  682.9 6.6 slice-start.2
  682.9 6.6 slice-start.3
  819.6 15.6 %copy-start.7 = (f32[512,19]{1,0:T(8,128)S(1)}, f32[512,19]{1,0:T(8,128)}, u32[]{:S(2)}) copy-start(f32[512,19]{1,0:T(8,128)} %fusion.57) | copy-start | bytes 116740
  819.6 15.8 %copy-start.20 = (f32[1,64,64]{2,1,0:T(8,128)S(1)}, f32[1,64,64]{2,1,0:T(8,128)}, u32[]{:S(2)}) copy-start(f32[1,64,64]{2,1,0:T(8,128)} %convolution_bitcast_fusion.1) | copy-start | bytes 49156
  819.6 15.8 %copy-start.21 = (f32[1,64,64]{2,1,0:T(8,128)S(1)}, f32[1,64,64]{2,1,0:T(8,128)}, u32[]{:S(2)}) copy-start(f32[1,64,64]{2,1,0:T(8,128)} %convolution_bitcast_fusion.2) | copy-start | bytes 49156
  819.6 15.8 %copy-start.22 = (f32[1,64,64]{2,1,0:T(8,128)S(1)}, f32[1,64,64]{2,1,0:T(8,128)}, u32[]{:S(2)}) copy-start(f32[1,64,64]{2,1,0:T(8,128)} %convolution_bitcast_fusion.3) | copy-start | bytes 49156
  819.6 15.8 %copy-start.14 = (f32[1,64,64]{2,1,0:T(8,128)S(1)}, f32[1,64,64]{2,1,0:T(8,128)}, u32[]{:S(2)}) copy-start(f32[1,64,64]{2,1,0:T(8,128)} %convolution_bitcast_fusion.4) | copy-start | bytes 49156
  819.7 15.8 %copy-start.15 = (f32[1,64,64]{2,1,0:T(8,128)S(1)}, f32[1,64,64]{2,1,0:T(8,128)}, u32[]{:S(2)}) copy-start(f32[1,64,64]{2,1,0:T(8,128)} %convolution_bitcast_fusion.5) | copy-start | bytes 49156
  819.7 15.8 %copy-start.16 = (f32[1,64,64]{2,1,0:T(8,128)S(1)}, f32[1,64,64]{2,1,0:T(8,128)}, u32[]{:S(2)}) copy-start(f32[1,64,64]{2,1,0:T(8,128)} %convolution_bitcast_fusion.6) | copy-start | bytes 49156
  819.7 15.8 %copy-start.17 = (f32[1,64,64]{2,1,0:T(8,128)S(1)}, f32[1,64,64]{2,1,0:T(8,128)}, u32[]{:S(2)}) copy-start(f32[1,64,64]{2,1,0:T(8,128)} %convolution_bitcast_fusion.7) | copy-start | bytes 49156
  819.7 15.8 %copy-start.18 = (f32[1,64,64]{2,1,0:T(8,128)S(1)}, f32[1,64,64]{2,1,0:T(8,128)}, u32[]{:S(2)}) copy-start(f32[1,64,64]{2,1,0:T(8,128)} %convolution_bitcast_fusion.8) | copy-start | bytes 49156
  819.7 15.8 %copy-start.19 = (f32[1,64,64]{2,1,0:T(8,128)S(1)}, f32[1,64,64]{2,1,0:T(8,128)}, u32[]{:S(2)}) copy-start(f32[1,64,64]{2,1,0:T(8,128)} %convolution_bitcast_fusion.9) | copy-start | bytes 49156
  835.7 7.3 copy-start.11
  835.7 7.3 copy-start.12
  835.7 7.3 copy-start.13
  835.7 8.0 copy-start.32
  835.7 8.0 copy-start.38
  835.7 8.0 copy-start.40
  835.8 8.0 copy-start.42
  906.1 1.0 copy-start.9
  906.1 1.1 copy-start.10
  906.1 149.3 %copy-start.4 = (f32[105984]{0:T(1024)S(1)}, f32[105984]{0:T(1024)}, u32[]{:S(2)}) copy-start(f32[105984]{0:T(1024)} %param.23) | copy-start | bytes 1271812
  906.1 151.5 %copy-start.25 = (f32[1,4,128]{2,1,0:T(4,128)S(1)}, f32[1,4,128]{2,1,0:T(4,128)}, u32[]{:S(2)}) copy-start(f32[1,4,128]{2,1,0:T(4,128)} %param.18) | copy-start | bytes 6148
  906.1 151.5 %copy-start.28 = (f32[128,4]{0,1:T(4,128)S(1)}, f32[128,4]{0,1:T(4,128)}, u32[]{:S(2)}) copy-start(f32[128,4]{0,1:T(4,128)} %copy-done.26) | copy-start | bytes 6148
  906.1 151.5 %copy-start.31 = (f32[512]{0:T(512)S(1)}, f32[512]{0:T(512)}, u32[]{:S(2)}) copy-start(f32[512]{0:T(512)} %copy-done.30) | copy-start | bytes 6148
  906.1 151.5 %copy-start.33 = (f32[512]{0:T(512)S(1)}, f32[512]{0:T(512)}, u32[]{:S(2)}) copy-start(f32[512]{0:T(512)} %get-tuple-element.141) | copy-start | bytes 6148
  906.1 151.5 %copy-start.35 = (f32[1,4,128]{2,1,0:T(4,128)S(1)}, f32[1,4,128]{2,1,0:T(4,128)}, u32[]{:S(2)}) copy-start(f32[1,4,128]{2,1,0:T(4,128)} %param.22) | copy-start | bytes 6148
  906.1 151.5 %copy-start.36 = (f32[512,1]{0,1:T(1,128)S(1)}, f32[512,1]{0,1:T(1,128)}, u32[]{:S(2)}) copy-start(f32[512,1]{0,1:T(1,128)} %get-tuple-element.169) | copy-start | bytes 6148
  906.2 189.2 %all-reduce.21.cloned.1.call-start = ((), (), s32[]{:S(2)}) async-start(), calls=%async_computation.1 | async-start | bytes 851968 | tf_op jit(solution)/shard_map/psum | solution.py:275
  909.7 185.7 %copy-start.8 = (f32[105984]{0:T(1024)S(1)}, f32[105984]{0:T(1024)}, u32[]{:S(2)}) copy-start(f32[105984]{0:T(1024)} %param.26) | copy-start | bytes 1271812
Sparse Core Ops, SparseCore 0:
  906.2 143.8 all-reduce.18
  1057.7 26.5 all-reduce.20
